TPU v7x, 32 devices: a whole 2x2x4 slice. The times are simulated.
32 devices in a mesh: mode: 2 (over y), col: 16 (over z, x, core).
Axes of the slice: x: 2, y: 2, z: 4, core: 2. Of those that a mesh axis runs over, the one named last changes fastest.
Arguments:
- tensor: float32 [512, 16, 4096], P('mode', 'col'), may hold values from -15 to 15
- start_basis: float32 [512, 128], replicated, may hold values from -6 to 6
Outputs:
- factor: float32 [512, 512], replicated
- basis: float32 [512, 128], replicated
- core: float32 [128, 16, 4096], P(None, 'col', 'mode')
All inputs are finite; a program needn't handle non-finite values.
Results may differ from a plain program's by a relative error of at most 0.00018.
Values sent between devices are 32-bit elements; how exact they have to be, the bound alone decides.
A program may use at most 64 MiB of HBM per device.

v0:
```python
import jax
import jax.numpy as jnp
from jax import lax
from jax.sharding import PartitionSpec as P

POWER = 2


def matmul(left, right):
    return jnp.dot(left, right, precision=lax.Precision.HIGHEST, preferred_element_type=jnp.float32)


def orthonormal(image):
    small = jnp.linalg.cholesky(matmul(image.T, image))
    return jax.scipy.linalg.solve_triangular(small, image.T, lower=True).T


def per_device(tensor, start_basis):
    regrouped = lax.all_to_all(tensor, "mode", split_axis=2, concat_axis=0, tiled=True)
    rows = regrouped.shape[0]
    flat = regrouped.reshape(rows, -1)
    columns = flat.shape[1] * lax.axis_size("mode") * lax.axis_size("col")
    gram = matmul(flat, flat.T)
    total = lax.psum(gram, ("mode", "col"))
    factor = jnp.linalg.cholesky(total / columns)
    basis = start_basis
    for step in range(POWER):
        image = matmul(factor, matmul(factor.T, basis))
        basis = orthonormal(image)
    core = matmul(basis.T, flat).reshape(basis.shape[1], regrouped.shape[1], regrouped.shape[2])
    return (factor, basis, core)


def solution(mesh):
    in_specs = (P("mode", "col", None), P())
    out_specs = (P(), P(), P(None, "col", "mode"))
    return jax.shard_map(
        per_device, mesh=mesh, in_specs=in_specs, out_specs=out_specs, check_vma=False
    )
```

profile of v0, /device:TPU:0, one launch (start us, length us, event | category | flops | bytes accessed | tf_op | source)
XLA Modules:
  0.0 377.8 jit_solution(11997995047091231864)
XLA Ops:
  7.2 0.0 copy-start
  7.2 0.0 all-reduce.3.cloned.1.call-start
  7.2 14.3 %copy.25 = f32[256,1,4096]{0,1,2:T(1,128)} copy(f32[256,1,4096]{2,1,0:T(1,128)} %param.5) | data formatting | bytes 8388608 | tf_op args[0]
  21.5 52.9 %all_to_all.15 = f32[256,1,4096]{0,1,2:T(1,128)S(1)} all-to-all(f32[256,1,4096]{0,1,2:T(1,128)} %copy.25), channel_id=1, replica_groups=mesh['mode'=2,'col'=16] {'mode'}, dimensions={2} | all-to-all | bytes 8388608 | tf_op jit(solution)/shard_map/all_to_all | solution.py:19
  74.4 2.2 copy.34
  76.7 5.4 %copy.26 = f32[2,256,1,2048]{3,1,0,2:T(8,128)} copy(f32[2,256,1,2048]{1,3,0,2:T(8,128)} %bitcast.71) | data formatting | bytes 8388608 | tf_op jit(solution)/shard_map/all_to_all | solution.py:19
  82.1 10.3 %fusion.22 = f32[512,512]{0,1:T(8,128)} fusion(f32[512,2048]{1,0:T(8,128)} %bitcast.69), kind=kOutput, calls=%fused_computation.57 | convolution fusion | flops 6442450944 | bytes 5242880 | tf_op jit(solution)/shard_map/dot_general | solution.py:10
  92.4 0.0 all-reduce.3.cloned.1.call-update
  92.4 131.3 %all-reduce.3.cloned.1.call-done = f32[512,512]{0,1:T(8,128)} async-done(((f32[512,512]{0,1:T(8,128)}), f32[512,512]{0,1:T(8,128)}) %all-reduce.3.cloned.1.call-update) | async-done | bytes 1048592 | tf_op jit(solution)/shard_map/psum | solution.py:24
  223.8 0.0 copy-start.2
  223.8 1.4 broadcast_multiply_fusion
  225.2 0.3 copy.28
  225.5 0.0 copy-done.2
  225.5 0.2 fusion
  225.8 11.7 %cholesky.120 = f32[128,128]{1,0:T(8,128)S(1)} custom-call(f32[128,128]{1,0:T(8,128)S(1)} %cholesky.330), custom_call_target="Cholesky" | custom-call | tf_op jit(solution)/shard_map/jit(cholesky)/cholesky | solution.py:25
  237.5 9.8 %custom-call.32 = f32[1,128,128]{1,2,0:T(8,128)S(1)} custom-call(f32[1,128,128]{2,1,0:T(8,128)S(1)} %get-tuple-element.26), custom_call_target="InvertDiagBlocksLowerTriangular" | custom-call | tf_op jit(solution)/shard_map/jit(cholesky)/cholesky | solution.py:25
  247.4 0.1 cholesky.251
  247.5 0.3 constant_dynamic-update-slice_fusion.2
  247.8 0.3 convolution_subtract_fusion
  248.2 11.7 %cholesky.244 = f32[128,128]{1,0:T(8,128)S(1)} custom-call(f32[128,128]{1,0:T(8,128)S(1)} %cholesky.334), custom_call_target="Cholesky" | custom-call | tf_op jit(solution)/shard_map/jit(cholesky)/cholesky | solution.py:25
  259.9 10.0 %custom-call.33 = f32[1,128,128]{1,2,0:T(8,128)S(1)} custom-call(f32[1,128,128]{2,1,0:T(8,128)S(1)} %get-tuple-element.23), custom_call_target="InvertDiagBlocksLowerTriangular" | custom-call | tf_op jit(solution)/shard_map/jit(cholesky)/cholesky | solution.py:25
  269.9 0.3 convolution_dynamic-update-slice_fusion
  270.2 0.4 convolution_subtract_fusion.1
  270.6 11.7 %cholesky.265 = f32[128,128]{1,0:T(8,128)S(1)} custom-call(f32[128,128]{1,0:T(8,128)S(1)} %cholesky.339), custom_call_target="Cholesky" | custom-call | tf_op jit(solution)/shard_map/jit(cholesky)/cholesky | solution.py:25
  282.3 0.6 compare_reduce_fusion.3
  283.0 9.8 %custom-call.34 = f32[1,128,128]{1,2,0:T(8,128)S(1)} custom-call(f32[1,128,128]{2,1,0:T(8,128)S(1)} %get-tuple-element.20), custom_call_target="InvertDiagBlocksLowerTriangular" | custom-call | tf_op jit(solution)/shard_map/jit(cholesky)/cholesky | solution.py:25
  292.8 0.2 convolution_dynamic-update-slice_fusion.1
  293.0 0.4 convolution_subtract_fusion.2
  293.4 11.7 %cholesky.282 = f32[128,128]{1,0:T(8,128)S(1)} custom-call(f32[128,128]{1,0:T(8,128)S(1)} %convolution_subtract_fusion.2), custom_call_target="Cholesky" | custom-call | tf_op jit(solution)/shard_map/jit(cholesky)/cholesky | solution.py:25
  305.1 0.7 compare_reduce_fusion.2
  305.8 0.6 compare_reduce_fusion.4
  309.4 0.1 select_select_fusion
  309.5 0.0 copy-done
  309.5 0.0 copy-start.1
  309.5 1.8 fusion.23
  311.3 1.0 fusion.24
  312.3 0.6 fusion.25
  312.9 0.1 copy.29
  313.0 11.7 %cholesky.310 = f32[128,128]{1,0:T(8,128)S(1)} custom-call(f32[128,128]{1,0:T(8,128)S(1)} %fusion.18), custom_call_target="Cholesky" | custom-call | tf_op jit(solution)/shard_map/jit(cholesky)/cholesky | solution.py:14
  324.8 0.6 compare_reduce_fusion.1
  325.4 0.7 fusion.11
  326.1 9.8 %custom-call.36 = f32[1,128,128]{1,2,0:T(8,128)S(1)} custom-call(f32[1,128,128]{2,1,0:T(8,128)S(1)} %fusion.11), custom_call_target="InvertDiagBlocksLowerTriangular" | custom-call | tf_op jit(solution)/shard_map/jit(_solve_triangular)/triangular_solve | solution.py:15
  335.9 0.4 fusion.4
  336.3 1.8 fusion.26
  338.1 1.2 fusion.27
  339.3 0.6 fusion.28
  339.9 0.0 copy-done.1
  339.9 0.1 copy.30
  340.0 11.7 %cholesky.321 = f32[128,128]{1,0:T(8,128)S(1)} custom-call(f32[128,128]{1,0:T(8,128)S(1)} %fusion.16), custom_call_target="Cholesky" | custom-call | tf_op jit(solution)/shard_map/jit(cholesky)/cholesky | solution.py:14
  351.8 0.6 compare_reduce_fusion
  352.4 0.7 fusion.12
  353.1 9.8 %custom-call.37 = f32[1,128,128]{1,2,0:T(8,128)S(1)} custom-call(f32[1,128,128]{2,1,0:T(8,128)S(1)} %fusion.12), custom_call_target="InvertDiagBlocksLowerTriangular" | custom-call | tf_op jit(solution)/shard_map/jit(_solve_triangular)/triangular_solve | solution.py:15
  362.9 0.4 fusion.2
  363.3 4.6 %convolution_bitcast_fusion = f32[128,1,2048]{2,0,1:T(8,128)S(1)} fusion(f32[128,512]{1,0:T(8,128)S(1)} %fusion.2, f32[512,2048]{1,0:T(8,128)} %bitcast.70), kind=kOutput, calls=%fused_computation | convolution fusion | flops 1610612736 | bytes 5505024 | tf_op jit(solution)/shard_map/dot_general | solution.py:10
  367.9 2.0 copy.32
  369.9 0.8 copy.31
  (11 shorter events, 0.3 us)
Async XLA Ops:
  7.2 302.3 %copy-start = (f32[512,128]{1,0:T(8,128)S(1)}, f32[512,128]{1,0:T(8,128)}, u32[]{:S(2)}) copy-start(f32[512,128]{1,0:T(8,128)} %param.6) | copy-start | bytes 786436
  7.2 216.6 %all-reduce.3.cloned.1.call-start = ((), (), s32[]{:S(2)}) async-start(), calls=%async_computation.1 | async-start | bytes 2097152 | tf_op jit(solution)/shard_map/psum | solution.py:24
  223.8 1.8 copy-start.2
  309.5 30.4 %copy-start.1 = (f32[512,512]{1,0:T(8,128)}, f32[512,512]{1,0:T(8,128)S(1)}, u32[]{:S(2)}) copy-start(f32[512,512]{1,0:T(8,128)S(1)} %select_select_fusion) | copy-start | bytes 3145732
Sparse Core Ops, SparseCore 0:
  92.6 131.1 all-reduce.2
where the time goes:
time: 382 us; the launch traced here: 378 us
  waiting for transfers between devices  131 us (34%)
  other arithmetic  126 us (33%)
  blocking collectives  52.9 us (14%)
  local copies, waits for them, and re-layouts  25.4 us (7%)
  matrix products  24.6 us (6%)
  between operations  17.5 us (5%)
    psum x1, waiting for transfers between devices, per_device(): total = lax.psum(gram, ('mode', 'col'))  131 us
    another operation x14, other arithmetic, per_device(): factor = jnp.linalg.cholesky(total / columns)  78.5 us
    all_to_all x1, blocking collectives, per_device(): lax.all_to_all(tensor, 'mode', split_axis=2, concat_axis=0, tiled=True)  52.9 us
    another operation x6, other arithmetic, orthonormal(): small = jnp.linalg.cholesky(matmul(image.T, image))  24.8 us
    dot_general x8, matrix products, matmul(): jnp.dot(left, right, precision=lax.Precision.HIGHEST, preferred_element_t...  21.9 us
    another operation x4, other arithmetic, orthonormal(): return jax.scipy.linalg.solve_triangular(small, image.T, lower=True).T  20.9 us
    unnamed x10, local copies, waits for them, and re-layouts  19.4 us
  transfers between devices with their start and end apart: 1, of which 1 were waited for; matrix products, arithmetic and copies ran while one was open for 0% of the time, Pallas kernels for 0%

commit v1 on v0

--- a/solution.py
+++ b/solution.py
@@ -21,7 +21,7 @@
     flat = regrouped.reshape(rows, -1)
     columns = flat.shape[1] * lax.axis_size("mode") * lax.axis_size("col")
     gram = matmul(flat, flat.T)
-    total = lax.psum(gram, ("mode", "col"))
+    total = jnp.sum(lax.all_gather(gram, ("mode", "col")), axis=0)
     factor = jnp.linalg.cholesky(total / columns)
     basis = start_basis
     for step in range(POWER):

time: 382 us -> 457 us (1.20)
  waiting for transfers between devices: 131 us -> 195 us
  other arithmetic: 126 us -> 137 us
    all_gather x0 -> x1, waiting for transfers between devices: none -> 195 us  [per_device(): total = jnp.sum(lax.all_gather(gram, ('mode', 'col')), axis=0)]
    psum x1 -> x0, waiting for transfers between devices: 131 us -> none  [per_device(): total = lax.psum(gram, ('mode', 'col'))]
    reduce_sum x0 -> x1, other arithmetic: none -> 12.4 us  [per_device(): total = jnp.sum(lax.all_gather(gram, ('mode', 'col')), axis=0)]
    unnamed x10 -> x8, local copies, waits for them, and re-layouts: 19.4 us -> 19.4 us
where the time goes in v1:
time: 457 us; the launch traced here: 452 us
  waiting for transfers between devices  195 us (43%)
  other arithmetic  137 us (30%)
  blocking collectives  52.9 us (12%)
  local copies, waits for them, and re-layouts  25.4 us (6%)
  matrix products  24.9 us (5%)
  between operations  17.1 us (4%)
    all_gather x1, waiting for transfers between devices, per_device(): total = jnp.sum(lax.all_gather(gram, ('mode', 'col')), axis=0)  195 us
    another operation x14, other arithmetic, per_device(): factor = jnp.linalg.cholesky(total / columns)  78.6 us
    all_to_all x1, blocking collectives, per_device(): lax.all_to_all(tensor, 'mode', split_axis=2, concat_axis=0, tiled=True)  52.9 us
    another operation x6, other arithmetic, orthonormal(): small = jnp.linalg.cholesky(matmul(image.T, image))  24.8 us
    dot_general x8, matrix products, matmul(): jnp.dot(left, right, precision=lax.Precision.HIGHEST, preferred_element_t...  22.2 us
    another operation x4, other arithmetic, orthonormal(): return jax.scipy.linalg.solve_triangular(small, image.T, lower=True).T  20.9 us
    unnamed x8, local copies, waits for them, and re-layouts  19.4 us
    reduce_sum x1, other arithmetic, per_device(): total = jnp.sum(lax.all_gather(gram, ('mode', 'col')), axis=0)  12.4 us
  transfers between devices with their start and end apart: 1, of which 1 were waited for; matrix products, arithmetic and copies ran while one was open for 0% of the time, Pallas kernels for 0%

profile of v1, /device:TPU:0, one launch (start us, length us, event | category | flops | bytes accessed | tf_op | source)
XLA Modules:
  0.0 452.4 jit_solution(16015458273392011050)
XLA Ops:
  7.2 0.0 copy-start
  7.2 0.0 all-gather.3.cloned.1.call-start
  7.2 14.3 %copy.22 = f32[256,1,4096]{0,1,2:T(1,128)} copy(f32[256,1,4096]{2,1,0:T(1,128)} %param.5) | data formatting | bytes 8388608 | tf_op args[0]
  21.5 52.9 %all_to_all.15 = f32[256,1,4096]{0,1,2:T(1,128)S(1)} all-to-all(f32[256,1,4096]{0,1,2:T(1,128)} %copy.22), channel_id=1, replica_groups=mesh['mode'=2,'col'=16] {'mode'}, dimensions={2} | all-to-all | bytes 8388608 | tf_op jit(solution)/shard_map/all_to_all | solution.py:19
  74.4 2.2 copy.29
  76.6 5.4 %copy.23 = f32[2,256,1,2048]{3,1,0,2:T(8,128)} copy(f32[2,256,1,2048]{1,3,0,2:T(8,128)} %bitcast.73) | data formatting | bytes 8388608 | tf_op jit(solution)/shard_map/all_to_all | solution.py:19
  82.0 10.3 %fusion.22 = f32[512,512]{1,0:T(8,128)} fusion(f32[512,2048]{1,0:T(8,128)} %bitcast.70), kind=kOutput, calls=%fused_computation.56 | convolution fusion | flops 6442450944 | bytes 5242880 | tf_op jit(solution)/shard_map/dot_general | solution.py:10
  92.3 0.0 all-gather.3.cloned.1.call-update
  92.3 194.9 %all-gather.3.cloned.1.call-done = f32[16384,512]{1,0:T(8,128)} async-done(((f32[512,512]{1,0:T(8,128)}), f32[16384,512]{1,0:T(8,128)}) %all-gather.3.cloned.1.call-update) | async-done | bytes 33554448 | tf_op jit(solution)/shard_map/all_gather | solution.py:24
  287.2 12.4 %reduce_sum.11 = f32[512,512]{1,0:T(8,128)S(1)} reduce(f32[32,512,512]{2,1,0:T(8,128)} %bitcast.72, f32[]{:T(128)} %constant.164.clone.1), dimensions={0}, to_apply=%region_0.0 | reduce | flops 8126464 | bytes 34603012 | tf_op jit(solution)/shard_map/reduce_sum | solution.py:24
  299.6 0.3 copy.24
  300.0 0.2 fusion
  300.2 11.7 %cholesky.120 = f32[128,128]{1,0:T(8,128)S(1)} custom-call(f32[128,128]{1,0:T(8,128)S(1)} %cholesky.330), custom_call_target="Cholesky" | custom-call | tf_op jit(solution)/shard_map/jit(cholesky)/cholesky | solution.py:25
  312.0 0.1 cholesky.251
  312.1 9.8 %custom-call.32 = f32[1,128,128]{1,2,0:T(8,128)S(1)} custom-call(f32[1,128,128]{2,1,0:T(8,128)S(1)} %get-tuple-element.26), custom_call_target="InvertDiagBlocksLowerTriangular" | custom-call | tf_op jit(solution)/shard_map/jit(cholesky)/cholesky | solution.py:25
  321.9 0.3 constant_dynamic-update-slice_fusion.2
  322.2 0.3 convolution_subtract_fusion
  322.6 11.7 %cholesky.244 = f32[128,128]{1,0:T(8,128)S(1)} custom-call(f32[128,128]{1,0:T(8,128)S(1)} %cholesky.334), custom_call_target="Cholesky" | custom-call | tf_op jit(solution)/shard_map/jit(cholesky)/cholesky | solution.py:25
  334.3 10.0 %custom-call.33 = f32[1,128,128]{1,2,0:T(8,128)S(1)} custom-call(f32[1,128,128]{2,1,0:T(8,128)S(1)} %get-tuple-element.23), custom_call_target="InvertDiagBlocksLowerTriangular" | custom-call | tf_op jit(solution)/shard_map/jit(cholesky)/cholesky | solution.py:25
  344.3 0.3 convolution_dynamic-update-slice_fusion
  344.6 0.4 convolution_subtract_fusion.1
  345.0 11.7 %cholesky.265 = f32[128,128]{1,0:T(8,128)S(1)} custom-call(f32[128,128]{1,0:T(8,128)S(1)} %cholesky.339), custom_call_target="Cholesky" | custom-call | tf_op jit(solution)/shard_map/jit(cholesky)/cholesky | solution.py:25
  356.8 0.6 compare_reduce_fusion.3
  357.4 9.8 %custom-call.34 = f32[1,128,128]{1,2,0:T(8,128)S(1)} custom-call(f32[1,128,128]{2,1,0:T(8,128)S(1)} %get-tuple-element.20), custom_call_target="InvertDiagBlocksLowerTriangular" | custom-call | tf_op jit(solution)/shard_map/jit(cholesky)/cholesky | solution.py:25
  367.2 0.2 convolution_dynamic-update-slice_fusion.1
  367.4 0.4 convolution_subtract_fusion.2
  367.8 11.7 %cholesky.282 = f32[128,128]{1,0:T(8,128)S(1)} custom-call(f32[128,128]{1,0:T(8,128)S(1)} %convolution_subtract_fusion.2), custom_call_target="Cholesky" | custom-call | tf_op jit(solution)/shard_map/jit(cholesky)/cholesky | solution.py:25
  379.6 0.7 compare_reduce_fusion.2
  380.3 0.6 compare_reduce_fusion.4
  383.6 0.1 select_select_fusion
  383.7 0.0 copy-done
  383.7 0.0 copy-start.1
  383.7 2.2 fusion.23
  385.9 1.0 fusion.24
  386.9 0.6 fusion.25
  387.5 0.1 copy.25
  387.6 11.7 %cholesky.310 = f32[128,128]{1,0:T(8,128)S(1)} custom-call(f32[128,128]{1,0:T(8,128)S(1)} %fusion.18), custom_call_target="Cholesky" | custom-call | tf_op jit(solution)/shard_map/jit(cholesky)/cholesky | solution.py:14
  399.4 0.6 compare_reduce_fusion.1
  400.0 0.7 fusion.11
  400.7 9.8 %custom-call.36 = f32[1,128,128]{1,2,0:T(8,128)S(1)} custom-call(f32[1,128,128]{2,1,0:T(8,128)S(1)} %fusion.11), custom_call_target="InvertDiagBlocksLowerTriangular" | custom-call | tf_op jit(solution)/shard_map/jit(_solve_triangular)/triangular_solve | solution.py:15
  410.5 0.4 fusion.4
  410.9 1.8 fusion.26
  412.7 1.2 fusion.27
  413.9 0.6 fusion.28
  414.5 0.0 copy-done.1
  414.5 0.1 copy.26
  414.6 11.7 %cholesky.321 = f32[128,128]{1,0:T(8,128)S(1)} custom-call(f32[128,128]{1,0:T(8,128)S(1)} %fusion.16), custom_call_target="Cholesky" | custom-call | tf_op jit(solution)/shard_map/jit(cholesky)/cholesky | solution.py:14
  426.4 0.6 compare_reduce_fusion
  427.0 0.7 fusion.12
  427.7 9.8 %custom-call.37 = f32[1,128,128]{1,2,0:T(8,128)S(1)} custom-call(f32[1,128,128]{2,1,0:T(8,128)S(1)} %fusion.12), custom_call_target="InvertDiagBlocksLowerTriangular" | custom-call | tf_op jit(solution)/shard_map/jit(_solve_triangular)/triangular_solve | solution.py:15
  437.5 0.4 fusion.2
  437.9 4.5 %convolution_bitcast_fusion = f32[128,1,2048]{2,0,1:T(8,128)S(1)} fusion(f32[128,512]{1,0:T(8,128)S(1)} %fusion.2, f32[512,2048]{1,0:T(8,128)} %bitcast.71), kind=kOutput, calls=%fused_computation | convolution fusion | flops 1610612736 | bytes 5505024 | tf_op jit(solution)/shard_map/dot_general | solution.py:10
  442.5 2.0 copy.28
  444.5 0.8 copy.27
  (11 shorter events, 0.3 us)
Async XLA Ops:
  7.2 376.5 %copy-start = (f32[512,128]{1,0:T(8,128)S(1)}, f32[512,128]{1,0:T(8,128)}, u32[]{:S(2)}) copy-start(f32[512,128]{1,0:T(8,128)} %param.6) | copy-start | bytes 786436
  7.2 280.0 %all-gather.3.cloned.1.call-start = ((), (), s32[]{:S(2)}) async-start(), calls=%async_computation.1 | async-start | bytes 34603008 | tf_op jit(solution)/shard_map/all_gather | solution.py:24
  383.7 30.8 %copy-start.1 = (f32[512,512]{1,0:T(8,128)}, f32[512,512]{1,0:T(8,128)S(1)}, u32[]{:S(2)}) copy-start(f32[512,512]{1,0:T(8,128)S(1)} %select_select_fusion) | copy-start | bytes 3145732
Sparse Core Ops, SparseCore 0:
  92.4 194.7 all-gather.2
